TPU v7x, 512 devices: a whole 4x4x16 slice. The times are simulated.
512 devices in a mesh: sub: 512 (over y, z, x, core).
Axes of the slice: x: 4, y: 4, z: 16, core: 2. Of those that a mesh axis runs over, the one named last changes fastest.
Arguments:
- right_side: bfloat16 [512, 1024, 128], P('sub'), may hold values from -6 to 6
- schur: bfloat16 [512, 1024, 1024], P('sub'), may hold values from -1 to 2
- neumann: bfloat16 [512, 1024, 1024], P('sub'), may hold values from -1 to 1
- weights: float32 [512, 1024], P('sub'), may hold values from 0.25 to 1
- neighbours: int32 [512, 4], P('sub'), may hold values from -1 to 511, as said below
- counts: int32 [512], P('sub'), may hold values from 512 to 1024, as said below
- shared_rows: int32 [512, 4, 128], P('sub'), may hold values from 0 to 1023, as said below
Outputs:
- solution: float32 [512, 1024, 128], P('sub')
Inputs may be any that keep to these rules, and one draw needn't show every extreme that they name: `neighbours`: slot 0 holds s + 1, slot 1 s - 1, slot 2 s + 16, slot 3 s - 16 where that link exists, else -1; links are symmetric: s names t in a slot exactly when t names s in the opposite slot. Subdomains 512 - 2 and 511 are always linked. `counts`: every subdomain has at least 512 nodes in use; some subdomain uses all 1024. `shared_rows`: every entry of subdomain s is below counts[s]; entries of one list may repeat.
All inputs are finite; a program needn't handle non-finite values.
Results may differ from a plain program's by a relative error of at most 0.0075.
Values may be sent and summed in bfloat16 or wider, within the bound.
A program may use at most 64 MiB of HBM per device.

v0:
```python
import jax
import jax.numpy as jnp
from jax import lax
from jax.sharding import PartitionSpec as P

ITERS = 4


link_offsets = (1, -1, 16, -16)
opposite_slot = (1, 0, 3, 2)
damping_factor = 0.7


def from_behind(block, axis, distance):
    devices = range(lax.axis_size(axis))
    route = [(i - distance, i) for i in devices if i - distance in devices]
    return lax.ppermute(block, axis, route)


def schur_product(s_mat, current):
    return lax.dot_general(
        s_mat, current, (((0,), (0,)), ((), ())), preferred_element_type=jnp.float32
    )


def neumann_product(n_mat, scaled):
    return jnp.dot(n_mat, scaled, preferred_element_type=jnp.float32)


def select_rows(picker, block):
    return lax.dot_general(
        picker, block, (((0,), (0,)), ((), ())), preferred_element_type=jnp.float32
    ).astype(jnp.bfloat16)


def body(right_side, schur, neumann, weights, neighbours, counts, shared_rows):
    rhs = right_side[0].astype(jnp.float32)
    s_mat = schur[0]
    n_mat = neumann[0]
    weight = weights[0][:, None]
    live = (neighbours[0] >= 0).astype(jnp.bfloat16)
    count = counts[0]
    links = shared_rows[0]
    width = s_mat.shape[0]
    share = links.shape[1]
    mask = (jnp.arange(width) < count).astype(jnp.float32)[:, None]
    positions = jnp.arange(width)[:, None]

    def one_hot(rows):
        return (positions == rows[None, :]).astype(jnp.bfloat16)

    placer = jnp.concatenate([one_hot(links[slot]) * live[slot] for slot in range(4)], 1)
    own_picker = jnp.concatenate([one_hot(links[opposite_slot[slot]]) for slot in range(4)], 1)

    def assemble(own, sent):
        received = []
        packed_all = select_rows(own_picker, sent)
        for slot in (0, 1):
            packed = packed_all[slot * share : (slot + 1) * share]
            received.append(from_behind(packed, "sub", -link_offsets[slot]))
        for slot in (2, 3):
            packed = packed_all[slot * share : (slot + 1) * share]
            received.append(from_behind(packed, "sub", -link_offsets[slot]))
        stacked = jnp.concatenate(received, 0)
        return own + jnp.dot(placer, stacked, preferred_element_type=jnp.float32)

    solution = jnp.zeros(rhs.shape, jnp.float32)
    for step in range(ITERS):
        current = solution.astype(jnp.bfloat16)
        local = mask * (rhs - schur_product(s_mat, current))
        residual = assemble(local, local.astype(jnp.bfloat16))
        scaled = (weight * residual).astype(jnp.bfloat16)
        correction = neumann_product(n_mat, scaled)
        weighted = mask * weight * correction
        update = assemble(weighted, weighted.astype(jnp.bfloat16))
        solution = solution + damping_factor * update
    return solution[None]


def solution(mesh):
    in_specs = (
        P("sub", None, None),
        P("sub", None, None),
        P("sub", None, None),
        P("sub", None),
        P("sub", None),
        P("sub"),
        P("sub", None, None),
    )
    out_specs = P("sub", None, None)
    return jax.shard_map(body, mesh=mesh, in_specs=in_specs, out_specs=out_specs, check_vma=False)
```

profile of v0, /device:TPU:24, one launch (start us, length us, event | category | flops | bytes accessed | tf_op | source)
XLA Modules:
  0.0 213.5 jit_solution(2662311374835953775)
XLA Ops:
  4.2 13.2 %collective-permute-start = (bf16[128,128]{1,0:T(8,128)(2,1)S(1)}, bf16[128,128]{1,0:T(8,128)(2,1)S(1)}, u32[]{:S(2)}, u32[]{:S(2)}) collective-permute-start(bf16[128,128]{1,0:T(8,128)(2,1)S(1)} %get-tuple-element.33), channel_id=1, source_target_pairs={{1,0},{2,1},{3,2},{4,3},{5,4},{6,5},{7,6},{8,7},{9,8},{10,9},{11,1... | collective-permute-start | bytes 98312 | tf_op jit(solution)/shard_map/ppermute | solution.py:17
  19.4 6.9 %collective-permute-start.2 = (bf16[128,128]{1,0:T(8,128)(2,1)S(1)}, bf16[128,128]{1,0:T(8,128)(2,1)S(1)}, u32[]{:S(2)}, u32[]{:S(2)}) collective-permute-start(bf16[128,128]{1,0:T(8,128)(2,1)S(1)} %get-tuple-element.35), channel_id=1, source_target_pairs={{16,0},{17,1},{18,2},{19,3},{20,4},{21,5},{22,6},{23,7},{24,8},{25... | collective-permute-start | bytes 98312 | tf_op jit(solution)/shard_map/ppermute | solution.py:17
  28.9 2.2 %broadcast_select_fusion = (bf16[1024,128]{1,0:T(8,128)(2,1)}, bf16[1024,128]{1,0:T(8,128)(2,1)}) fusion(bf16[]{:T(256)} %bitcast.12, s32[128]{0:T(128)S(1)} %get-tuple-element.39, bf16[]{:T(256)} %bitcast.10, s32[128]{0:T(128)S(1)} %get-tuple-element.40), kind=kLoop, calls=%fused_computation.161 | loop fusion | flops 524288 | bytes 525316 | tf_op jit(solution)/shard_map/mul | solution.py:52
  31.1 2.2 %broadcast_select_fusion.2 = (bf16[1024,128]{1,0:T(8,128)(2,1)}, bf16[1024,128]{1,0:T(8,128)(2,1)}) fusion(bf16[]{:T(256)} %bitcast.8, s32[128]{0:T(128)S(1)} %get-tuple-element.37, bf16[]{:T(256)} %bitcast.6, s32[128]{0:T(128)S(1)} %get-tuple-element.38), kind=kLoop, calls=%fused_computation.163 | loop fusion | flops 524288 | bytes 525316 | tf_op jit(solution)/shard_map/mul | solution.py:52
  33.3 2.5 %collective-permute-done.1 = bf16[128,128]{1,0:T(8,128)(2,1)S(1)} collective-permute-done((bf16[128,128]{1,0:T(8,128)(2,1)S(1)}, bf16[128,128]{1,0:T(8,128)(2,1)S(1)}, u32[]{:S(2)}, u32[]{:S(2)}) %collective-permute-start.1) | collective-permute-done | bytes 32800 | tf_op jit(solution)/shard_map/ppermute | solution.py:17
  36.4 3.9 %fusion.83 = f32[1024,128]{0,1:T(8,128)} fusion(bf16[1,1024,1024]{2,1,0:T(8,128)(2,1)} %param.9, f32[1024,128]{0,1:T(8,128)S(1)} %fusion.77, f32[1024]{0:T(1024)S(1)} %bitcast.115, f32[1024]{0:T(1024)S(1)} %fusion.233, bf16[128,128]{1,0:T(8,128)(2,1)S(1)} %collective-permute-done.3, bf16[128,128]{1,0:T(8,128)(2,1)S(1)} %collective-permute-done.2, ...), kind=kOutput, calls=%fused_computation.66 | convolution fusion | flops 407896064 | bytes 4333568 | tf_op jit(solution)/shard_map/dot_general | solution.py:27
  42.1 5.4 %collective-permute-start.4 = (bf16[128,128]{1,0:T(8,128)(2,1)S(1)}, bf16[128,128]{1,0:T(8,128)(2,1)S(1)}, u32[]{:S(2)}, u32[]{:S(2)}) collective-permute-start(bf16[128,128]{1,0:T(8,128)(2,1)S(1)} %get-tuple-element.29), channel_id=1, source_target_pairs={{1,0},{2,1},{3,2},{4,3},{5,4},{6,5},{7,6},{8,7},{9,8},{10,9},{11,1... | collective-permute-start | bytes 98312 | tf_op jit(solution)/shard_map/ppermute | solution.py:17
  49.5 6.9 %collective-permute-start.6 = (bf16[128,128]{1,0:T(8,128)(2,1)S(1)}, bf16[128,128]{1,0:T(8,128)(2,1)S(1)}, u32[]{:S(2)}, u32[]{:S(2)}) collective-permute-start(bf16[128,128]{1,0:T(8,128)(2,1)S(1)} %get-tuple-element.31), channel_id=1, source_target_pairs={{16,0},{17,1},{18,2},{19,3},{20,4},{21,5},{22,6},{23,7},{24,8},{25... | collective-permute-start | bytes 98312 | tf_op jit(solution)/shard_map/ppermute | solution.py:17
  58.4 7.5 %collective-permute-done.5 = bf16[128,128]{1,0:T(8,128)(2,1)S(1)} collective-permute-done((bf16[128,128]{1,0:T(8,128)(2,1)S(1)}, bf16[128,128]{1,0:T(8,128)(2,1)S(1)}, u32[]{:S(2)}, u32[]{:S(2)}) %collective-permute-start.5) | collective-permute-done | bytes 32800 | tf_op jit(solution)/shard_map/ppermute | solution.py:17
  72.1 6.9 %collective-permute-start.10 = (bf16[128,128]{1,0:T(8,128)(2,1)S(1)}, bf16[128,128]{1,0:T(8,128)(2,1)S(1)}, u32[]{:S(2)}, u32[]{:S(2)}) collective-permute-start(bf16[128,128]{1,0:T(8,128)(2,1)S(1)} %get-tuple-element.27), channel_id=1, source_target_pairs={{16,0},{17,1},{18,2},{19,3},{20,4},{21,5},{22,6},{23,7},{24,8},{25... | collective-permute-start | bytes 98312 | tf_op jit(solution)/shard_map/ppermute | solution.py:17
  81.0 7.6 %collective-permute-done.9 = bf16[128,128]{1,0:T(8,128)(2,1)} collective-permute-done((bf16[128,128]{1,0:T(8,128)(2,1)S(1)}, bf16[128,128]{1,0:T(8,128)(2,1)}, u32[]{:S(2)}, u32[]{:S(2)}) %collective-permute-start.9) | collective-permute-done | bytes 32800 | tf_op jit(solution)/shard_map/ppermute | solution.py:17
  88.6 4.1 %fusion.89 = f32[1024,128]{0,1:T(8,128)} fusion(bf16[1,1024,1024]{2,1,0:T(8,128)(2,1)} %param.9, f32[1024,128]{0,1:T(8,128)} %copy-done.4, f32[1024]{0:T(1024)S(1)} %bitcast.116, f32[1024]{0:T(1024)S(1)} %fusion.233, bf16[128,128]{1,0:T(8,128)(2,1)S(1)} %collective-permute-done.11, bf16[128,128]{1,0:T(8,128)(2,1)S(1)} %collective-permute-done.10, ...), kind=kOutput, calls=%fused_computation.68 | convolution fusion | flops 407896064 | bytes 4333568 | tf_op jit(solution)/shard_map/dot_general | solution.py:27
  98.4 6.9 %collective-permute-start.14 = (bf16[128,128]{1,0:T(8,128)(2,1)S(1)}, bf16[128,128]{1,0:T(8,128)(2,1)S(1)}, u32[]{:S(2)}, u32[]{:S(2)}) collective-permute-start(bf16[128,128]{1,0:T(8,128)(2,1)S(1)} %get-tuple-element.23), channel_id=1, source_target_pairs={{16,0},{17,1},{18,2},{19,3},{20,4},{21,5},{22,6},{23,7},{24,8},{25... | collective-permute-start | bytes 98312 | tf_op jit(solution)/shard_map/ppermute | solution.py:17
  107.3 7.8 %collective-permute-done.13 = bf16[128,128]{1,0:T(8,128)(2,1)S(1)} collective-permute-done((bf16[128,128]{1,0:T(8,128)(2,1)S(1)}, bf16[128,128]{1,0:T(8,128)(2,1)S(1)}, u32[]{:S(2)}, u32[]{:S(2)}) %collective-permute-start.13) | collective-permute-done | bytes 32800 | tf_op jit(solution)/shard_map/ppermute | solution.py:17
  120.6 6.9 %collective-permute-start.18 = (bf16[128,128]{1,0:T(8,128)(2,1)S(1)}, bf16[128,128]{1,0:T(8,128)(2,1)S(1)}, u32[]{:S(2)}, u32[]{:S(2)}) collective-permute-start(bf16[128,128]{1,0:T(8,128)(2,1)S(1)} %get-tuple-element.19), channel_id=1, source_target_pairs={{16,0},{17,1},{18,2},{19,3},{20,4},{21,5},{22,6},{23,7},{24,8},{25... | collective-permute-start | bytes 98312 | tf_op jit(solution)/shard_map/ppermute | solution.py:17
  129.5 7.6 %collective-permute-done.17 = bf16[128,128]{1,0:T(8,128)(2,1)} collective-permute-done((bf16[128,128]{1,0:T(8,128)(2,1)S(1)}, bf16[128,128]{1,0:T(8,128)(2,1)}, u32[]{:S(2)}, u32[]{:S(2)}) %collective-permute-start.17) | collective-permute-done | bytes 32800 | tf_op jit(solution)/shard_map/ppermute | solution.py:17
  137.1 3.9 %fusion.95 = f32[1024,128]{0,1:T(8,128)} fusion(bf16[1,1024,1024]{2,1,0:T(8,128)(2,1)} %param.9, f32[1024,128]{0,1:T(8,128)S(1)} %fusion.65, f32[1024]{0:T(1024)S(1)} %bitcast.117, f32[1024]{0:T(1024)S(1)} %fusion.233, bf16[128,128]{1,0:T(8,128)(2,1)S(1)} %collective-permute-done.19, bf16[128,128]{1,0:T(8,128)(2,1)S(1)} %collective-permute-done.18, ...), kind=kOutput, calls=%fused_computation.70 | convolution fusion | flops 407896064 | bytes 4333568 | tf_op jit(solution)/shard_map/dot_general | solution.py:27
  146.7 6.9 %collective-permute-start.22 = (bf16[128,128]{1,0:T(8,128)(2,1)S(1)}, bf16[128,128]{1,0:T(8,128)(2,1)S(1)}, u32[]{:S(2)}, u32[]{:S(2)}) collective-permute-start(bf16[128,128]{1,0:T(8,128)(2,1)S(1)} %get-tuple-element.15), channel_id=1, source_target_pairs={{16,0},{17,1},{18,2},{19,3},{20,4},{21,5},{22,6},{23,7},{24,8},{25... | collective-permute-start | bytes 98312 | tf_op jit(solution)/shard_map/ppermute | solution.py:17
  155.6 7.5 %collective-permute-done.21 = bf16[128,128]{1,0:T(8,128)(2,1)S(1)} collective-permute-done((bf16[128,128]{1,0:T(8,128)(2,1)S(1)}, bf16[128,128]{1,0:T(8,128)(2,1)S(1)}, u32[]{:S(2)}, u32[]{:S(2)}) %collective-permute-start.21) | collective-permute-done | bytes 32800 | tf_op jit(solution)/shard_map/ppermute | solution.py:17
  169.4 6.9 %collective-permute-start.26 = (bf16[128,128]{1,0:T(8,128)(2,1)S(1)}, bf16[128,128]{1,0:T(8,128)(2,1)S(1)}, u32[]{:S(2)}, u32[]{:S(2)}) collective-permute-start(bf16[128,128]{1,0:T(8,128)(2,1)S(1)} %get-tuple-element.11), channel_id=1, source_target_pairs={{16,0},{17,1},{18,2},{19,3},{20,4},{21,5},{22,6},{23,7},{24,8},{25... | collective-permute-start | bytes 98312 | tf_op jit(solution)/shard_map/ppermute | solution.py:17
  178.3 7.6 %collective-permute-done.25 = bf16[128,128]{1,0:T(8,128)(2,1)} collective-permute-done((bf16[128,128]{1,0:T(8,128)(2,1)S(1)}, bf16[128,128]{1,0:T(8,128)(2,1)}, u32[]{:S(2)}, u32[]{:S(2)}) %collective-permute-start.25) | collective-permute-done | bytes 32800 | tf_op jit(solution)/shard_map/ppermute | solution.py:17
  185.9 4.0 %fusion.101 = f32[1024,128]{0,1:T(8,128)} fusion(bf16[1,1024,1024]{2,1,0:T(8,128)(2,1)} %param.9, f32[1024,128]{0,1:T(8,128)} %copy-done.3, f32[1024]{0:T(1024)S(1)} %bitcast.118, f32[1024]{0:T(1024)S(1)} %fusion.233, bf16[128,128]{1,0:T(8,128)(2,1)S(1)} %collective-permute-done.27, bf16[128,128]{1,0:T(8,128)(2,1)S(1)} %collective-permute-done.26, ...), kind=kOutput, calls=%fused_computation.72 | convolution fusion | flops 407896064 | bytes 4333568 | tf_op jit(solution)/shard_map/dot_general | solution.py:27
  195.6 6.9 %collective-permute-start.30 = (bf16[128,128]{1,0:T(8,128)(2,1)S(1)}, bf16[128,128]{1,0:T(8,128)(2,1)S(1)}, u32[]{:S(2)}, u32[]{:S(2)}) collective-permute-start(bf16[128,128]{1,0:T(8,128)(2,1)S(1)} %get-tuple-element.7), channel_id=1, source_target_pairs={{16,0},{17,1},{18,2},{19,3},{20,4},{21,5},{22,6},{23,7},{24,8},{25... | collective-permute-start | bytes 98312 | tf_op jit(solution)/shard_map/ppermute | solution.py:17
  204.5 7.5 %collective-permute-done.29 = bf16[128,128]{1,0:T(8,128)(2,1)S(1)} collective-permute-done((bf16[128,128]{1,0:T(8,128)(2,1)S(1)}, bf16[128,128]{1,0:T(8,128)(2,1)S(1)}, u32[]{:S(2)}, u32[]{:S(2)}) %collective-permute-start.29) | collective-permute-done | bytes 32800 | tf_op jit(solution)/shard_map/ppermute | solution.py:17
  (136 shorter events, 61.9 us)
Async XLA Ops:
  4.2 29.1 %collective-permute-start = (bf16[128,128]{1,0:T(8,128)(2,1)S(1)}, bf16[128,128]{1,0:T(8,128)(2,1)S(1)}, u32[]{:S(2)}, u32[]{:S(2)}) collective-permute-start(bf16[128,128]{1,0:T(8,128)(2,1)S(1)} %get-tuple-element.33), channel_id=1, source_target_pairs={{1,0},{2,1},{3,2},{4,3},{5,4},{6,5},{7,6},{8,7},{9,8},{10,9},{11,1... | collective-permute-start | bytes 98312 | tf_op jit(solution)/shard_map/ppermute | solution.py:17
  17.4 15.8 %collective-permute-start.3 = (bf16[128,128]{1,0:T(8,128)(2,1)S(1)}, bf16[128,128]{1,0:T(8,128)(2,1)S(1)}, u32[]{:S(2)}, u32[]{:S(2)}) collective-permute-start(bf16[128,128]{1,0:T(8,128)(2,1)S(1)} %get-tuple-element.34), channel_id=1, source_target_pairs={{0,16},{1,17},{2,18},{3,19},{4,20},{5,21},{6,22},{7,23},{8,24},{9,... | collective-permute-start | bytes 98312 | tf_op jit(solution)/shard_map/ppermute | solution.py:17
  19.4 13.9 %collective-permute-start.2 = (bf16[128,128]{1,0:T(8,128)(2,1)S(1)}, bf16[128,128]{1,0:T(8,128)(2,1)S(1)}, u32[]{:S(2)}, u32[]{:S(2)}) collective-permute-start(bf16[128,128]{1,0:T(8,128)(2,1)S(1)} %get-tuple-element.35), channel_id=1, source_target_pairs={{16,0},{17,1},{18,2},{19,3},{20,4},{21,5},{22,6},{23,7},{24,8},{25... | collective-permute-start | bytes 98312 | tf_op jit(solution)/shard_map/ppermute | solution.py:17
  26.3 9.5 %collective-permute-start.1 = (bf16[128,128]{1,0:T(8,128)(2,1)S(1)}, bf16[128,128]{1,0:T(8,128)(2,1)S(1)}, u32[]{:S(2)}, u32[]{:S(2)}) collective-permute-start(bf16[128,128]{1,0:T(8,128)(2,1)S(1)} %get-tuple-element.36), channel_id=1, source_target_pairs={{0,1},{1,2},{2,3},{3,4},{4,5},{5,6},{6,7},{7,8},{8,9},{9,10},{10,1... | collective-permute-start | bytes 98312 | tf_op jit(solution)/shard_map/ppermute | solution.py:17
  42.1 16.2 %collective-permute-start.4 = (bf16[128,128]{1,0:T(8,128)(2,1)S(1)}, bf16[128,128]{1,0:T(8,128)(2,1)S(1)}, u32[]{:S(2)}, u32[]{:S(2)}) collective-permute-start(bf16[128,128]{1,0:T(8,128)(2,1)S(1)} %get-tuple-element.29), channel_id=1, source_target_pairs={{1,0},{2,1},{3,2},{4,3},{5,4},{6,5},{7,6},{8,7},{9,8},{10,9},{11,1... | collective-permute-start | bytes 98312 | tf_op jit(solution)/shard_map/ppermute | solution.py:17
  47.5 10.8 %collective-permute-start.7 = (bf16[128,128]{1,0:T(8,128)(2,1)S(1)}, bf16[128,128]{1,0:T(8,128)(2,1)S(1)}, u32[]{:S(2)}, u32[]{:S(2)}) collective-permute-start(bf16[128,128]{1,0:T(8,128)(2,1)S(1)} %get-tuple-element.30), channel_id=1, source_target_pairs={{0,16},{1,17},{2,18},{3,19},{4,20},{5,21},{6,22},{7,23},{8,24},{9,... | collective-permute-start | bytes 98312 | tf_op jit(solution)/shard_map/ppermute | solution.py:17
  56.4 9.5 %collective-permute-start.5 = (bf16[128,128]{1,0:T(8,128)(2,1)S(1)}, bf16[128,128]{1,0:T(8,128)(2,1)S(1)}, u32[]{:S(2)}, u32[]{:S(2)}) collective-permute-start(bf16[128,128]{1,0:T(8,128)(2,1)S(1)} %get-tuple-element.32), channel_id=1, source_target_pairs={{0,1},{1,2},{2,3},{3,4},{4,5},{5,6},{6,7},{7,8},{8,9},{9,10},{10,1... | collective-permute-start | bytes 98312 | tf_op jit(solution)/shard_map/ppermute | solution.py:17
  68.2 12.7 %collective-permute-start.8 = (bf16[128,128]{1,0:T(8,128)(2,1)S(1)}, bf16[128,128]{1,0:T(8,128)(2,1)S(1)}, u32[]{:S(2)}, u32[]{:S(2)}) collective-permute-start(bf16[128,128]{1,0:T(8,128)(2,1)S(1)} %get-tuple-element.25), channel_id=1, source_target_pairs={{1,0},{2,1},{3,2},{4,3},{5,4},{6,5},{7,6},{8,7},{9,8},{10,9},{11,1... | collective-permute-start | bytes 98312 | tf_op jit(solution)/shard_map/ppermute | solution.py:17
  70.2 10.8 %collective-permute-start.11 = (bf16[128,128]{1,0:T(8,128)(2,1)S(1)}, bf16[128,128]{1,0:T(8,128)(2,1)S(1)}, u32[]{:S(2)}, u32[]{:S(2)}) collective-permute-start(bf16[128,128]{1,0:T(8,128)(2,1)S(1)} %get-tuple-element.26), channel_id=1, source_target_pairs={{0,16},{1,17},{2,18},{3,19},{4,20},{5,21},{6,22},{7,23},{8,24},{9,... | collective-permute-start | bytes 98312 | tf_op jit(solution)/shard_map/ppermute | solution.py:17
  79.0 9.6 %collective-permute-start.9 = (bf16[128,128]{1,0:T(8,128)(2,1)S(1)}, bf16[128,128]{1,0:T(8,128)(2,1)}, u32[]{:S(2)}, u32[]{:S(2)}) collective-permute-start(bf16[128,128]{1,0:T(8,128)(2,1)S(1)} %get-tuple-element.28), channel_id=1, source_target_pairs={{0,1},{1,2},{2,3},{3,4},{4,5},{5,6},{6,7},{7,8},{8,9},{9,10},{10,1... | collective-permute-start | bytes 98312 | tf_op jit(solution)/shard_map/ppermute | solution.py:17
  94.6 12.7 %collective-permute-start.12 = (bf16[128,128]{1,0:T(8,128)(2,1)S(1)}, bf16[128,128]{1,0:T(8,128)(2,1)S(1)}, u32[]{:S(2)}, u32[]{:S(2)}) collective-permute-start(bf16[128,128]{1,0:T(8,128)(2,1)S(1)} %get-tuple-element.21), channel_id=1, source_target_pairs={{1,0},{2,1},{3,2},{4,3},{5,4},{6,5},{7,6},{8,7},{9,8},{10,9},{11,1... | collective-permute-start | bytes 98312 | tf_op jit(solution)/shard_map/ppermute | solution.py:17
  96.5 10.8 %collective-permute-start.15 = (bf16[128,128]{1,0:T(8,128)(2,1)S(1)}, bf16[128,128]{1,0:T(8,128)(2,1)S(1)}, u32[]{:S(2)}, u32[]{:S(2)}) collective-permute-start(bf16[128,128]{1,0:T(8,128)(2,1)S(1)} %get-tuple-element.22), channel_id=1, source_target_pairs={{0,16},{1,17},{2,18},{3,19},{4,20},{5,21},{6,22},{7,23},{8,24},{9,... | collective-permute-start | bytes 98312 | tf_op jit(solution)/shard_map/ppermute | solution.py:17
  105.4 9.7 %collective-permute-start.13 = (bf16[128,128]{1,0:T(8,128)(2,1)S(1)}, bf16[128,128]{1,0:T(8,128)(2,1)S(1)}, u32[]{:S(2)}, u32[]{:S(2)}) collective-permute-start(bf16[128,128]{1,0:T(8,128)(2,1)S(1)} %get-tuple-element.24), channel_id=1, source_target_pairs={{0,1},{1,2},{2,3},{3,4},{4,5},{5,6},{6,7},{7,8},{8,9},{9,10},{10,1... | collective-permute-start | bytes 98312 | tf_op jit(solution)/shard_map/ppermute | solution.py:17
  116.7 12.7 %collective-permute-start.16 = (bf16[128,128]{1,0:T(8,128)(2,1)S(1)}, bf16[128,128]{1,0:T(8,128)(2,1)S(1)}, u32[]{:S(2)}, u32[]{:S(2)}) collective-permute-start(bf16[128,128]{1,0:T(8,128)(2,1)S(1)} %get-tuple-element.17), channel_id=1, source_target_pairs={{1,0},{2,1},{3,2},{4,3},{5,4},{6,5},{7,6},{8,7},{9,8},{10,9},{11,1... | collective-permute-start | bytes 98312 | tf_op jit(solution)/shard_map/ppermute | solution.py:17
  118.6 10.8 %collective-permute-start.19 = (bf16[128,128]{1,0:T(8,128)(2,1)S(1)}, bf16[128,128]{1,0:T(8,128)(2,1)S(1)}, u32[]{:S(2)}, u32[]{:S(2)}) collective-permute-start(bf16[128,128]{1,0:T(8,128)(2,1)S(1)} %get-tuple-element.18), channel_id=1, source_target_pairs={{0,16},{1,17},{2,18},{3,19},{4,20},{5,21},{6,22},{7,23},{8,24},{9,... | collective-permute-start | bytes 98312 | tf_op jit(solution)/shard_map/ppermute | solution.py:17
  127.5 9.6 %collective-permute-start.17 = (bf16[128,128]{1,0:T(8,128)(2,1)S(1)}, bf16[128,128]{1,0:T(8,128)(2,1)}, u32[]{:S(2)}, u32[]{:S(2)}) collective-permute-start(bf16[128,128]{1,0:T(8,128)(2,1)S(1)} %get-tuple-element.20), channel_id=1, source_target_pairs={{0,1},{1,2},{2,3},{3,4},{4,5},{5,6},{6,7},{7,8},{8,9},{9,10},{10,1... | collective-permute-start | bytes 98312 | tf_op jit(solution)/shard_map/ppermute | solution.py:17
  142.9 12.7 %collective-permute-start.20 = (bf16[128,128]{1,0:T(8,128)(2,1)S(1)}, bf16[128,128]{1,0:T(8,128)(2,1)S(1)}, u32[]{:S(2)}, u32[]{:S(2)}) collective-permute-start(bf16[128,128]{1,0:T(8,128)(2,1)S(1)} %get-tuple-element.13), channel_id=1, source_target_pairs={{1,0},{2,1},{3,2},{4,3},{5,4},{6,5},{7,6},{8,7},{9,8},{10,9},{11,1... | collective-permute-start | bytes 98312 | tf_op jit(solution)/shard_map/ppermute | solution.py:17
  144.8 10.8 %collective-permute-start.23 = (bf16[128,128]{1,0:T(8,128)(2,1)S(1)}, bf16[128,128]{1,0:T(8,128)(2,1)S(1)}, u32[]{:S(2)}, u32[]{:S(2)}) collective-permute-start(bf16[128,128]{1,0:T(8,128)(2,1)S(1)} %get-tuple-element.14), channel_id=1, source_target_pairs={{0,16},{1,17},{2,18},{3,19},{4,20},{5,21},{6,22},{7,23},{8,24},{9,... | collective-permute-start | bytes 98312 | tf_op jit(solution)/shard_map/ppermute | solution.py:17
  153.7 9.5 %collective-permute-start.21 = (bf16[128,128]{1,0:T(8,128)(2,1)S(1)}, bf16[128,128]{1,0:T(8,128)(2,1)S(1)}, u32[]{:S(2)}, u32[]{:S(2)}) collective-permute-start(bf16[128,128]{1,0:T(8,128)(2,1)S(1)} %get-tuple-element.16), channel_id=1, source_target_pairs={{0,1},{1,2},{2,3},{3,4},{4,5},{5,6},{6,7},{7,8},{8,9},{9,10},{10,1... | collective-permute-start | bytes 98312 | tf_op jit(solution)/shard_map/ppermute | solution.py:17
  165.5 12.7 %collective-permute-start.24 = (bf16[128,128]{1,0:T(8,128)(2,1)S(1)}, bf16[128,128]{1,0:T(8,128)(2,1)S(1)}, u32[]{:S(2)}, u32[]{:S(2)}) collective-permute-start(bf16[128,128]{1,0:T(8,128)(2,1)S(1)} %get-tuple-element.9), channel_id=1, source_target_pairs={{1,0},{2,1},{3,2},{4,3},{5,4},{6,5},{7,6},{8,7},{9,8},{10,9},{11,1... | collective-permute-start | bytes 98312 | tf_op jit(solution)/shard_map/ppermute | solution.py:17
  167.5 10.8 %collective-permute-start.27 = (bf16[128,128]{1,0:T(8,128)(2,1)S(1)}, bf16[128,128]{1,0:T(8,128)(2,1)S(1)}, u32[]{:S(2)}, u32[]{:S(2)}) collective-permute-start(bf16[128,128]{1,0:T(8,128)(2,1)S(1)} %get-tuple-element.10), channel_id=1, source_target_pairs={{0,16},{1,17},{2,18},{3,19},{4,20},{5,21},{6,22},{7,23},{8,24},{9,... | collective-permute-start | bytes 98312 | tf_op jit(solution)/shard_map/ppermute | solution.py:17
  176.3 9.6 %collective-permute-start.25 = (bf16[128,128]{1,0:T(8,128)(2,1)S(1)}, bf16[128,128]{1,0:T(8,128)(2,1)}, u32[]{:S(2)}, u32[]{:S(2)}) collective-permute-start(bf16[128,128]{1,0:T(8,128)(2,1)S(1)} %get-tuple-element.12), channel_id=1, source_target_pairs={{0,1},{1,2},{2,3},{3,4},{4,5},{5,6},{6,7},{7,8},{8,9},{9,10},{10,1... | collective-permute-start | bytes 98312 | tf_op jit(solution)/shard_map/ppermute | solution.py:17
  191.8 12.7 %collective-permute-start.28 = (bf16[128,128]{1,0:T(8,128)(2,1)S(1)}, bf16[128,128]{1,0:T(8,128)(2,1)S(1)}, u32[]{:S(2)}, u32[]{:S(2)}) collective-permute-start(bf16[128,128]{1,0:T(8,128)(2,1)S(1)} %get-tuple-element.5), channel_id=1, source_target_pairs={{1,0},{2,1},{3,2},{4,3},{5,4},{6,5},{7,6},{8,7},{9,8},{10,9},{11,1... | collective-permute-start | bytes 98312 | tf_op jit(solution)/shard_map/ppermute | solution.py:17
  193.7 10.8 %collective-permute-start.31 = (bf16[128,128]{1,0:T(8,128)(2,1)S(1)}, bf16[128,128]{1,0:T(8,128)(2,1)S(1)}, u32[]{:S(2)}, u32[]{:S(2)}) collective-permute-start(bf16[128,128]{1,0:T(8,128)(2,1)S(1)} %get-tuple-element.6), channel_id=1, source_target_pairs={{0,16},{1,17},{2,18},{3,19},{4,20},{5,21},{6,22},{7,23},{8,24},{9,... | collective-permute-start | bytes 98312 | tf_op jit(solution)/shard_map/ppermute | solution.py:17
  (36 other events, 614.6 us)
where the time goes:
time: 215 us; the launch traced here: 214 us
  starting transfers between devices  116 us (54%)
  waiting for transfers between devices  55.6 us (26%)
  matrix products  29.3 us (14%)
  local copies, waits for them, and re-layouts  5.97 us (3%)
  other arithmetic  4.7 us (2%)
    ppermute x32, starting transfers between devices, from_behind(): return lax.ppermute(block, axis, route)  116 us
    ppermute x32, waiting for transfers between devices, from_behind(): return lax.ppermute(block, axis, route)  55.6 us
    dot_general x4, matrix products, neumann_product(): return jnp.dot(n_mat, scaled, preferred_element_type=jnp.float32)  16 us
    dot_general x8, matrix products, select_rows(): lax.dot_general(picker, block, (((0,), (0,)), ((), ())), preferred_elemen...  9.56 us
    mul x2, other arithmetic, body(): one_hot(links[slot]) * live[slot]  4.34 us
  transfers between devices with their start and end apart: 32, of which 8 were waited for; matrix products, arithmetic and copies ran while one was open for 2% of the time, Pallas kernels for 0%

commit v1 on v0

v1 whole, which is shorter than its diff:
```python
import functools

import jax
import jax.numpy as jnp
from jax import lax
from jax.experimental import pallas as pl
from jax.experimental.pallas import tpu as pltpu
from jax.sharding import PartitionSpec as P

ITERS = 4
OFFSETS = (1, -1, 16, -16)
OPPOSITE = (1, 0, 3, 2)
SEND_ORDER = (2, 3, 0, 1)
DAMPING = 0.7
F32, BF16 = jnp.float32, jnp.bfloat16


def mm(a, b):
    return jnp.dot(a, b, preferred_element_type=F32)


def mm_t(a, b):
    return lax.dot_general(a, b, (((1,), (1,)), ((), ())), preferred_element_type=F32)


def kernel(
    n, rhs_hbm, s_hbm, n_hbm, w_ref, nb_ref, cnt_ref, rows_ref, out_ref,
    rhs, s_mat, n_mat, st, et, el, gs, gse, gn, gne, wm, w_e, p0, t, x, u, wlb,
    send, recv, load_sem, send_sem, recv_sem,
):
    width, leads = rhs.shape
    share = rows_ref.shape[2]
    links = 4 * share
    me = lax.axis_index("sub")
    partner = [lax.rem(me + (o + n), n) for o in OFFSETS]

    loads = [
        pltpu.make_async_copy(rhs_hbm.at[0], rhs, load_sem.at[0]),
        pltpu.make_async_copy(n_hbm.at[0], n_mat, load_sem.at[1]),
        pltpu.make_async_copy(s_hbm.at[0], s_mat, load_sem.at[2]),
    ]
    for copy in loads:
        copy.start()

    barrier = pltpu.get_barrier_semaphore()
    for to in partner:
        pl.semaphore_signal(barrier, inc=1, device_id=(to,), device_id_type=pl.DeviceIdType.MESH)

    def copy_of(e, slot):
        there = OPPOSITE[slot]
        return pltpu.make_async_remote_copy(
            src_ref=send.at[e, pl.ds(slot * share, share)],
            dst_ref=recv.at[e, pl.ds(there * share, share)],
            send_sem=send_sem.at[e, slot],
            recv_sem=recv_sem.at[e, there],
            device_id=(partner[slot],),
            device_id_type=pl.DeviceIdType.MESH,
        )

    def part(slot):
        return slice(slot * share, (slot + 1) * share)

    row_of = lax.broadcasted_iota(jnp.int32, (width, share), 0)
    lane_of = lax.broadcasted_iota(jnp.int32, (share, width), 1)
    for slot in range(4):
        rows = rows_ref[0, slot : slot + 1, :]
        column = jnp.transpose(jnp.broadcast_to(rows, (share, share)))[:, :1]
        hit = lane_of == column
        et[part(slot), :] = hit.astype(F32).astype(BF16)
        live = (nb_ref[0, slot] >= 0).astype(F32)
        el[:, part(slot)] = (jnp.where(row_of == rows, 1.0, 0.0) * live).astype(BF16)
        mine = jnp.sum(jnp.where(hit, w_ref[0:1, :], 0.0), axis=1, keepdims=True)
        w_e[part(slot), :] = jnp.broadcast_to(mine, (share, leads))

    loads[0].wait()
    first = mm(et[...], rhs[...])
    p0[...] = first
    send[0] = first.astype(BF16)
    pl.semaphore_wait(barrier, 4)
    for slot in SEND_ORDER:
        copy_of(0, slot).start()

    count = cnt_ref[0]
    for block in range(width // 128):
        at = slice(block * 128, (block + 1) * 128)
        w_col = jnp.transpose(jnp.broadcast_to(w_ref[0:1, at], (128, 128)))
        used = lax.broadcasted_iota(jnp.int32, (128, 128), 0) + block * 128 < count
        wm[at, :] = jnp.where(used, w_col, 0.0)[:, :leads]

    t[...] = rhs[...].astype(F32)
    wlb[...] = (wm[...] * t[...]).astype(BF16)
    loads[1].wait()
    gn[...] = mm(et[...], n_mat[...]).astype(BF16)
    gne[...] = mm(gn[...], el[...]).astype(BF16)
    u[...] = mm(gn[...], wlb[...])
    x[...] = jnp.zeros_like(x)

    def second(e, first_time):
        for slot in SEND_ORDER:
            copy_of(e, slot).wait_recv()
        s1 = (w_e[...] * recv[e].astype(F32)).astype(BF16)
        send[e + 1] = (w_e[...] * (u[...] + mm(gne[...], s1))).astype(BF16)
        for slot in SEND_ORDER:
            copy_of(e + 1, slot).start()
        scaled = (wm[...] * (t[...] + mm(el[...], recv[e]))).astype(BF16)
        x[...] = x[...] + DAMPING * (wm[...] * mm(n_mat[...], scaled))
        if first_time:
            loads[2].wait()
            gs[...] = mm_t(et[...], s_mat[...]).astype(BF16)
            gse[...] = mm(gs[...], el[...]).astype(BF16)
        u[...] = p0[...] - mm(gs[...], x[...].astype(BF16))

    def third(e, first_time):
        for slot in SEND_ORDER:
            copy_of(e, slot).wait_recv()
        send[e + 1] = (u[...] - DAMPING * mm(gse[...], recv[e])).astype(BF16)
        for slot in SEND_ORDER:
            copy_of(e + 1, slot).start()
        x[...] = x[...] + DAMPING * mm(el[...], recv[e])
        if first_time:
            st[...] = jnp.transpose(s_mat[...])
        t[...] = rhs[...].astype(F32) - mm(st[...], x[...].astype(BF16))
        wlb[...] = (wm[...] * t[...]).astype(BF16)
        u[...] = mm(gn[...], wlb[...])

    for step in range(ITERS):
        second(2 * step, step == 0)
        if step < ITERS - 1:
            third(2 * step + 1, step == 0)
    last = 2 * ITERS - 1
    for slot in SEND_ORDER:
        copy_of(last, slot).wait_recv()
    out_ref[0] = x[...] + DAMPING * mm(el[...], recv[last])
    for e in range(2 * ITERS):
        for slot in SEND_ORDER:
            copy_of(e, slot).wait_send()


def body(right_side, schur, neumann, weights, neighbours, counts, shared_rows):
    n = lax.axis_size("sub")
    _, width, leads = right_side.shape
    share = shared_rows.shape[2]
    links = 4 * share
    hbm = pl.BlockSpec(memory_space=pl.ANY)
    vmem = pl.BlockSpec(memory_space=pltpu.VMEM)
    smem = pl.BlockSpec(memory_space=pltpu.SMEM)
    return pl.pallas_call(
        functools.partial(kernel, n),
        out_shape=jax.ShapeDtypeStruct((1, width, leads), F32),
        in_specs=[hbm, hbm, hbm, vmem, smem, smem, vmem],
        out_specs=vmem,
        scratch_shapes=[
            pltpu.VMEM((width, leads), BF16),
            pltpu.VMEM((width, width), BF16),
            pltpu.VMEM((width, width), BF16),
            pltpu.VMEM((width, width), BF16),
            pltpu.VMEM((links, width), BF16),
            pltpu.VMEM((width, links), BF16),
            pltpu.VMEM((links, width), BF16),
            pltpu.VMEM((links, links), BF16),
            pltpu.VMEM((links, width), BF16),
            pltpu.VMEM((links, links), BF16),
            pltpu.VMEM((width, leads), F32),
            pltpu.VMEM((links, leads), F32),
            pltpu.VMEM((links, leads), F32),
            pltpu.VMEM((width, leads), F32),
            pltpu.VMEM((width, leads), F32),
            pltpu.VMEM((links, leads), F32),
            pltpu.VMEM((width, leads), BF16),
            pltpu.VMEM((2 * ITERS, links, leads), BF16),
            pltpu.VMEM((2 * ITERS, links, leads), BF16),
            pltpu.SemaphoreType.DMA((3,)),
            pltpu.SemaphoreType.DMA((2 * ITERS, 4)),
            pltpu.SemaphoreType.DMA((2 * ITERS, 4)),
        ],
        compiler_params=pltpu.CompilerParams(
            collective_id=0, has_side_effects=True, vmem_limit_bytes=48 * 2**20
        ),
    )(right_side, schur, neumann, weights, neighbours, counts, shared_rows)


def solution(mesh):
    in_specs = (
        P("sub", None, None),
        P("sub", None, None),
        P("sub", None, None),
        P("sub", None),
        P("sub", None),
        P("sub"),
        P("sub", None, None),
    )
    return jax.shard_map(body, mesh=mesh, in_specs=in_specs, out_specs=P("sub", None, None), check_vma=False)
```

time: 215 us -> 70.1 us (0.33)
  the two profiles are of different devices: /device:TPU:24 before, /device:TPU:39 now
where the time goes in v1:
time: 70.1 us; the launch traced here: 69.9 us
  Pallas kernels  62.2 us (89%)
  local copies, waits for them, and re-layouts  6.94 us (10%)
    pallas_call x1, Pallas kernels, body(): pl.pallas_call(functools.partial(kernel, n), out_shape=jax.ShapeDtypeStru...  62.2 us
    unnamed x13, local copies, waits for them, and re-layouts  6.94 us

profile of v1, /device:TPU:39, one launch (start us, length us, event | category | flops | bytes accessed | tf_op | source)
XLA Modules:
  0.0 69.9 jit_solution(500385188630760972)
XLA Ops:
  0.7 0.0 copy-start
  0.7 1.6 %copy-done = bf16[1,1024,1024]{2,1,0:T(8,128)(2,1)S(1)} copy-done((bf16[1,1024,1024]{2,1,0:T(8,128)(2,1)S(1)}, bf16[1,1024,1024]{2,1,0:T(8,128)(2,1)}, u32[]{:S(2)}) %copy-start) | copy-done | bytes 2097176
  2.2 0.0 copy-start.1
  2.2 1.6 %copy-done.1 = bf16[1,1024,1024]{2,1,0:T(8,128)(2,1)S(1)} copy-done((bf16[1,1024,1024]{2,1,0:T(8,128)(2,1)S(1)}, bf16[1,1024,1024]{2,1,0:T(8,128)(2,1)}, u32[]{:S(2)}) %copy-start.1) | copy-done | bytes 2097176
  3.8 0.0 copy-start.2
  3.8 0.9 %copy-done.2 = bf16[1,1024,128]{2,1,0:T(8,128)(2,1)S(1)} copy-done((bf16[1,1024,128]{2,1,0:T(8,128)(2,1)S(1)}, bf16[1,1024,128]{2,1,0:T(8,128)(2,1)}, u32[]{:S(2)}) %copy-start.2) | copy-done | bytes 262168
  4.8 0.0 copy-start.3
  4.8 0.7 copy-done.3
  5.5 0.0 copy-start.4
  5.5 0.7 copy-done.4
  6.2 0.0 copy-start.5
  6.2 0.7 copy-done.5
  6.8 62.2 %shard_map.73 = f32[1,1024,128]{2,1,0:T(8,128)S(1)} custom-call(bf16[1,1024,128]{2,1,0:T(8,128)(2,1)S(1)} %copy-done.2, bf16[1,1024,1024]{2,1,0:T(8,128)(2,1)S(1)} %copy-done, bf16[1,1024,1024]{2,1,0:T(8,128)(2,1)S(1)} %copy-done.1, f32[1,1024]{1,0:T(1,128)S(1)} %copy-done.3, s32[1,4]{1,0:T(1,128)S(1)} %copy-done.5, s32[1]{0:T(128)S(6)} %copy.9.cnt_ref, ...), custom_call_target="tpu_custom_call" | custom-call | tf_op jit(solution)/shard_map/pallas_call | solution.py:147
  69.1 0.8 %copy.10 = f32[1,1024,128]{2,1,0:T(8,128)} copy(f32[1,1024,128]{2,1,0:T(8,128)S(1)} %shard_map.73) | data formatting | bytes 1048576
Async XLA Ops:
  0.7 1.6 %copy-start = (bf16[1,1024,1024]{2,1,0:T(8,128)(2,1)S(1)}, bf16[1,1024,1024]{2,1,0:T(8,128)(2,1)}, u32[]{:S(2)}) copy-start(bf16[1,1024,1024]{2,1,0:T(8,128)(2,1)} %s_hbm.1) | copy-start | bytes 6291460
  2.2 1.6 %copy-start.1 = (bf16[1,1024,1024]{2,1,0:T(8,128)(2,1)S(1)}, bf16[1,1024,1024]{2,1,0:T(8,128)(2,1)}, u32[]{:S(2)}) copy-start(bf16[1,1024,1024]{2,1,0:T(8,128)(2,1)} %n_hbm.1) | copy-start | bytes 6291460
  3.8 0.9 %copy-start.2 = (bf16[1,1024,128]{2,1,0:T(8,128)(2,1)S(1)}, bf16[1,1024,128]{2,1,0:T(8,128)(2,1)}, u32[]{:S(2)}) copy-start(bf16[1,1024,128]{2,1,0:T(8,128)(2,1)} %rhs_hbm.1) | copy-start | bytes 786436
  4.8 0.7 copy-start.3
  5.5 0.7 copy-start.4
  6.2 0.7 copy-start.5

commit v2 on v1

v2 whole, which is shorter than its diff:
```python
import functools

import jax
import jax.numpy as jnp
from jax import lax
from jax.experimental import pallas as pl
from jax.experimental.pallas import tpu as pltpu
from jax.sharding import PartitionSpec as P

ITERS = 4
OFFSETS = (1, -1, 16, -16)
OPPOSITE = (1, 0, 3, 2)
DAMPING = 0.7
CHUNKS = 2
F32, BF16 = jnp.float32, jnp.bfloat16


def mm(a, b):
    return jnp.dot(a, b, preferred_element_type=F32)


def mm_t(a, b):
    return lax.dot_general(a, b, (((1,), (1,)), ((), ())), preferred_element_type=F32)


def kernel(
    n, rhs_hbm, s_hbm, n_hbm, w_hbm, nb_hbm, cnt_hbm, rows_hbm, out_ref,
    rhs_in, s_mat, n_mat, w_in, nb_in, cnt_in, rows_in,
    rhs, nt, pick, place, gs, gse, gn, gne, w3, wm, w_e, p0, t, x, u, wlb,
    send, recv, load_sem, send_sem, recv_sem,
):
    leads, width = rhs.shape
    share = rows_in.shape[2]
    me = lax.axis_index("sub")
    partner = [lax.rem(me + (o + n), n) for o in OFFSETS]
    exists = [(me + o >= 0) & (me + o < n) for o in OFFSETS]

    def each(do):
        for slot in range(4):
            pl.when(exists[slot])(functools.partial(do, slot))

    pairs = [
        (rows_hbm, rows_in), (rhs_hbm.at[0], rhs_in), (w_hbm, w_in), (nb_hbm, nb_in),
        (cnt_hbm, cnt_in), (n_hbm.at[0], n_mat), (s_hbm.at[0], s_mat),
    ]
    loads = [pltpu.make_async_copy(a, b, load_sem.at[i]) for i, (a, b) in enumerate(pairs)]
    for copy in loads:
        copy.start()

    barrier = pltpu.get_barrier_semaphore()

    for slot in range(4):
        @pl.when(jnp.logical_not(exists[slot]))
        def _():
            for e in range(2 * ITERS):
                recv[e, slot] = jnp.zeros((leads, share), BF16)

    def greet(slot):
        pl.semaphore_signal(
            barrier, inc=1, device_id=(partner[slot],), device_id_type=pl.DeviceIdType.MESH
        )

    each(greet)

    step_rows = leads // CHUNKS

    def copy_of(e, c, slot, there):
        rows = pl.ds(c * step_rows, step_rows)
        return pltpu.make_async_remote_copy(
            src_ref=send.at[e, slot, rows],
            dst_ref=recv.at[e, there, rows],
            send_sem=send_sem.at[e, c, slot],
            recv_sem=recv_sem.at[e, c, there],
            device_id=(partner[slot],),
            device_id_type=pl.DeviceIdType.MESH,
        )

    def start(e, c):
        each(lambda slot: copy_of(e, c, slot, OPPOSITE[slot]).start())

    def arrive(e, c):
        each(lambda slot: copy_of(e, c, slot, slot).wait_recv())

    def put(e, c, rows):
        for slot in range(4):
            send[e, slot, pl.ds(c * step_rows, step_rows)] = rows[:, slot * share : (slot + 1) * share]

    def got(e, lo, hi):
        return jnp.concatenate([recv[e, slot, lo:hi] for slot in range(4)], axis=1)

    loads[0].wait()
    node_of = lax.broadcasted_iota(jnp.int32, (width, share), 0)
    for slot in range(4):
        hit = node_of == rows_in[0, slot : slot + 1, :]
        pick[:, slot * share : (slot + 1) * share] = hit.astype(F32).astype(BF16)
    loads[1].wait()
    rhs[...] = jnp.transpose(rhs_in[...])
    p0[...] = mm(rhs[...], pick[...])
    for c in range(CHUNKS):
        put(0, c, p0[c * step_rows : (c + 1) * step_rows].astype(BF16))
    pl.semaphore_wait(barrier, sum(jnp.where(there, 1, 0) for there in exists))
    for c in range(CHUNKS):
        start(0, c)

    for i in (2, 3, 4):
        loads[i].wait()
    node = lax.broadcasted_iota(jnp.int32, (1, width), 1)
    w = w_in[...]
    wm[...] = jnp.where(node < cnt_in[0], w, 0.0)
    high = w.astype(BF16)
    rest = w - high.astype(F32)
    middle = rest.astype(BF16)
    low = (rest - middle.astype(F32)).astype(BF16)
    term = lax.broadcasted_iota(jnp.int32, w3.shape, 0)
    w3[...] = jnp.where(
        term == 0, high.astype(F32), jnp.where(term == 1, middle.astype(F32), jnp.where(term == 2, low.astype(F32), 0.0))
    ).astype(BF16)
    w_e[...] = jnp.sum(mm(w3[...], pick[...]), axis=0, keepdims=True)
    lane_of = lax.broadcasted_iota(jnp.int32, (share, width), 1)
    for slot in range(4):
        rows = rows_in[0, slot : slot + 1, :]
        column = jnp.transpose(jnp.broadcast_to(rows, (share, share)))[:, :1]
        live = (nb_in[0, slot] >= 0).astype(F32)
        place[slot * share : (slot + 1) * share, :] = ((lane_of == column).astype(F32) * live).astype(BF16)

    t[...] = rhs[...].astype(F32)
    wlb[...] = (wm[...] * t[...]).astype(BF16)
    loads[5].wait()
    nt[...] = jnp.transpose(n_mat[...])
    gn[...] = mm(nt[...], pick[...]).astype(BF16)
    gne[...] = mm(place[...], gn[...]).astype(BF16)
    u[...] = mm(wlb[...], gn[...])
    x[...] = jnp.zeros_like(x)

    def spans():
        return [(c, c * step_rows, (c + 1) * step_rows) for c in range(CHUNKS)]

    def second(e, first_time):
        for c, lo, hi in spans():
            arrive(e, c)
            s1 = (w_e[...] * got(e, lo, hi).astype(F32)).astype(BF16)
            put(e + 1, c, (w_e[...] * (u[lo:hi] + mm(s1, gne[...]))).astype(BF16))
            start(e + 1, c)
        scaled = (wm[...] * (t[...] + mm(got(e, 0, leads), place[...]))).astype(BF16)
        x[...] = x[...] + DAMPING * (wm[...] * mm(scaled, nt[...]))
        if first_time:
            loads[6].wait()
            gs[...] = mm(s_mat[...], pick[...]).astype(BF16)
            gse[...] = mm(place[...], gs[...]).astype(BF16)

    def third(e):
        u[...] = p0[...] - mm(x[...].astype(BF16), gs[...])
        for c, lo, hi in spans():
            arrive(e, c)
            put(e + 1, c, (u[lo:hi] - DAMPING * mm(got(e, lo, hi), gse[...])).astype(BF16))
            start(e + 1, c)
        x[...] = x[...] + DAMPING * mm(got(e, 0, leads), place[...])
        t[...] = rhs[...].astype(F32) - mm(x[...].astype(BF16), s_mat[...])
        wlb[...] = (wm[...] * t[...]).astype(BF16)
        u[...] = mm(wlb[...], gn[...])

    for step in range(ITERS):
        second(2 * step, step == 0)
        if step < ITERS - 1:
            third(2 * step + 1)
    last = 2 * ITERS - 1
    out_ref[0] = jnp.transpose(x[...])
    for c in range(CHUNKS):
        arrive(last, c)
    kept = jnp.concatenate(
        [recv[last, slot].astype(F32) * (nb_in[0, slot] >= 0).astype(F32) for slot in range(4)], axis=1
    ).astype(BF16)
    out_ref[0] = out_ref[0] + DAMPING * mm_t(pick[...], kept)
    for e in range(2 * ITERS):
        for c in range(CHUNKS):
            each(lambda slot: copy_of(e, c, slot, OPPOSITE[slot]).wait_send())


def body(right_side, schur, neumann, weights, neighbours, counts, shared_rows):
    n = lax.axis_size("sub")
    _, width, leads = right_side.shape
    share = shared_rows.shape[2]
    links = 4 * share
    vmem = pl.BlockSpec(memory_space=pltpu.VMEM)
    return pl.pallas_call(
        functools.partial(kernel, n),
        out_shape=jax.ShapeDtypeStruct((1, width, leads), F32),
        in_specs=[pl.BlockSpec(memory_space=pltpu.HBM)] * 7,
        out_specs=vmem,
        scratch_shapes=[
            pltpu.VMEM((width, leads), BF16),
            pltpu.VMEM((width, width), BF16),
            pltpu.VMEM((width, width), BF16),
            pltpu.VMEM((1, width), F32),
            pltpu.SMEM((1, 4), jnp.int32),
            pltpu.SMEM((1,), jnp.int32),
            pltpu.VMEM((1, 4, share), jnp.int32),
            pltpu.VMEM((leads, width), BF16),
            pltpu.VMEM((width, width), BF16),
            pltpu.VMEM((width, links), BF16),
            pltpu.VMEM((links, width), BF16),
            pltpu.VMEM((width, links), BF16),
            pltpu.VMEM((links, links), BF16),
            pltpu.VMEM((width, links), BF16),
            pltpu.VMEM((links, links), BF16),
            pltpu.VMEM((16, width), BF16),
            pltpu.VMEM((1, width), F32),
            pltpu.VMEM((1, links), F32),
            pltpu.VMEM((leads, links), F32),
            pltpu.VMEM((leads, width), F32),
            pltpu.VMEM((leads, width), F32),
            pltpu.VMEM((leads, links), F32),
            pltpu.VMEM((leads, width), BF16),
            pltpu.VMEM((2 * ITERS, 4, leads, share), BF16),
            pltpu.VMEM((2 * ITERS, 4, leads, share), BF16),
            pltpu.SemaphoreType.DMA((7,)),
            pltpu.SemaphoreType.DMA((2 * ITERS, CHUNKS, 4)),
            pltpu.SemaphoreType.DMA((2 * ITERS, CHUNKS, 4)),
        ],
        compiler_params=pltpu.CompilerParams(
            collective_id=0, has_side_effects=True, vmem_limit_bytes=60 * 2**20
        ),
    )(right_side, schur, neumann, weights, neighbours, counts, shared_rows)


def solution(mesh):
    in_specs = (
        P("sub", None, None),
        P("sub", None, None),
        P("sub", None, None),
        P("sub", None),
        P("sub", None),
        P("sub"),
        P("sub", None, None),
    )
    return jax.shard_map(body, mesh=mesh, in_specs=in_specs, out_specs=P("sub", None, None), check_vma=False)
```

time: 70.1 us -> 56 us (0.80)
  the two profiles are of different devices: /device:TPU:39 before, /device:TPU:24 now
where the time goes in v2:
time: 56 us; the launch traced here: 55.9 us
  Pallas kernels  53.3 us (95%)
  local copies, waits for them, and re-layouts  1.87 us (3%)
  between operations  0.66 us (1%)
    pallas_call x1, Pallas kernels, body(): pl.pallas_call(functools.partial(kernel, n), out_shape=jax.ShapeDtypeStru...  53.3 us
    unnamed x1, local copies, waits for them, and re-layouts  1.87 us

profile of v2, /device:TPU:24, one launch (start us, length us, event | category | flops | bytes accessed | tf_op | source)
XLA Modules:
  0.0 55.9 jit_solution(3201887008883577741)
XLA Ops:
  0.7 53.3 %shard_map.73 = f32[1,1024,128]{2,1,0:T(8,128)} custom-call(bf16[1,1024,128]{2,1,0:T(8,128)(2,1)} %rhs_hbm.1, bf16[1,1024,1024]{2,1,0:T(8,128)(2,1)} %s_hbm.1, bf16[1,1024,1024]{2,1,0:T(8,128)(2,1)} %n_hbm.1, f32[1,1024]{1,0:T(1,128)} %w_hbm.1, s32[1,4]{1,0:T(1,128)} %nb_hbm.1, s32[1]{0:T(128)S(6)} %copy.9.cnt_hbm, s32[1,4,128]{2,1,0:T(4,128)} %rows_hbm.1), custom_call_target="tpu_custom_call" | custom-call | tf_op jit(solution)/shard_map/pallas_call | solution.py:185
  54.0 1.9 %copy.10 = f32[1,1024,128]{2,1,0:T(8,128)} copy(f32[1,1024,128]{2,1,0:T(8,128)} %shard_map.73) | data formatting | bytes 1048576

commit v3 on v2

--- a/solution.py
+++ b/solution.py
@@ -35,9 +35,18 @@
     partner = [lax.rem(me + (o + n), n) for o in OFFSETS]
     exists = [(me + o >= 0) & (me + o < n) for o in OFFSETS]
 
-    def each(do):
-        for slot in range(4):
+    def each(do, slots=range(4)):
+        for slot in slots:
             pl.when(exists[slot])(functools.partial(do, slot))
+
+    barrier = pltpu.get_barrier_semaphore()
+
+    def greet(slot):
+        pl.semaphore_signal(
+            barrier, inc=1, device_id=(partner[slot],), device_id_type=pl.DeviceIdType.MESH
+        )
+
+    each(greet)
 
     pairs = [
         (rows_hbm, rows_in), (rhs_hbm.at[0], rhs_in), (w_hbm, w_in), (nb_hbm, nb_in),
@@ -46,21 +55,6 @@
     loads = [pltpu.make_async_copy(a, b, load_sem.at[i]) for i, (a, b) in enumerate(pairs)]
     for copy in loads:
         copy.start()
-
-    barrier = pltpu.get_barrier_semaphore()
-
-    for slot in range(4):
-        @pl.when(jnp.logical_not(exists[slot]))
-        def _():
-            for e in range(2 * ITERS):
-                recv[e, slot] = jnp.zeros((leads, share), BF16)
-
-    def greet(slot):
-        pl.semaphore_signal(
-            barrier, inc=1, device_id=(partner[slot],), device_id_type=pl.DeviceIdType.MESH
-        )
-
-    each(greet)
 
     step_rows = leads // CHUNKS
 
@@ -75,15 +69,15 @@
             device_id_type=pl.DeviceIdType.MESH,
         )
 
-    def start(e, c):
-        each(lambda slot: copy_of(e, c, slot, OPPOSITE[slot]).start())
+    def start(e, c, slots=range(4)):
+        each(lambda slot: copy_of(e, c, slot, OPPOSITE[slot]).start(), slots)
 
     def arrive(e, c):
-        each(lambda slot: copy_of(e, c, slot, slot).wait_recv())
-
-    def put(e, c, rows):
-        for slot in range(4):
-            send[e, slot, pl.ds(c * step_rows, step_rows)] = rows[:, slot * share : (slot + 1) * share]
+        each(lambda slot: copy_of(e, c, slot, slot).wait_recv(), (2, 3, 0, 1))
+
+    def put(e, c, rows, slots=range(4)):
+        for i, slot in enumerate(slots):
+            send[e, slot, pl.ds(c * step_rows, step_rows)] = rows[:, i * share : (i + 1) * share]
 
     def got(e, lo, hi):
         return jnp.concatenate([recv[e, slot, lo:hi] for slot in range(4)], axis=1)
@@ -101,6 +95,12 @@
     pl.semaphore_wait(barrier, sum(jnp.where(there, 1, 0) for there in exists))
     for c in range(CHUNKS):
         start(0, c)
+
+    for slot in range(4):
+        @pl.when(jnp.logical_not(exists[slot]))
+        def _():
+            for e in range(2 * ITERS):
+                recv[e, slot] = jnp.zeros((leads, share), BF16)
 
     for i in (2, 3, 4):
         loads[i].wait()
@@ -135,12 +135,15 @@
     def spans():
         return [(c, c * step_rows, (c + 1) * step_rows) for c in range(CHUNKS)]
 
+    halves = [((0, 1), slice(0, 2 * share)), ((2, 3), slice(2 * share, 4 * share))]
+
     def second(e, first_time):
         for c, lo, hi in spans():
             arrive(e, c)
             s1 = (w_e[...] * got(e, lo, hi).astype(F32)).astype(BF16)
-            put(e + 1, c, (w_e[...] * (u[lo:hi] + mm(s1, gne[...]))).astype(BF16))
-            start(e + 1, c)
+            for slots, at in halves:
+                put(e + 1, c, (w_e[:, at] * (u[lo:hi, at] + mm(s1, gne[:, at]))).astype(BF16), slots)
+                start(e + 1, c, slots)
         scaled = (wm[...] * (t[...] + mm(got(e, 0, leads), place[...]))).astype(BF16)
         x[...] = x[...] + DAMPING * (wm[...] * mm(scaled, nt[...]))
         if first_time:
@@ -152,8 +155,10 @@
         u[...] = p0[...] - mm(x[...].astype(BF16), gs[...])
         for c, lo, hi in spans():
             arrive(e, c)
-            put(e + 1, c, (u[lo:hi] - DAMPING * mm(got(e, lo, hi), gse[...])).astype(BF16))
-            start(e + 1, c)
+            arrived = got(e, lo, hi)
+            for slots, at in halves:
+                put(e + 1, c, (u[lo:hi, at] - DAMPING * mm(arrived, gse[:, at])).astype(BF16), slots)
+                start(e + 1, c, slots)
         x[...] = x[...] + DAMPING * mm(got(e, 0, leads), place[...])
         t[...] = rhs[...].astype(F32) - mm(x[...].astype(BF16), s_mat[...])
         wlb[...] = (wm[...] * t[...]).astype(BF16)
@@ -174,6 +179,10 @@
     for e in range(2 * ITERS):
         for c in range(CHUNKS):
             each(lambda slot: copy_of(e, c, slot, OPPOSITE[slot]).wait_send())
+
+
+def in_hbm(*arrays):
+    return [pltpu.with_memory_space_constraint(a, pltpu.HBM) for a in arrays]
 
 
 def body(right_side, schur, neumann, weights, neighbours, counts, shared_rows):
@@ -218,9 +227,9 @@
             pltpu.SemaphoreType.DMA((2 * ITERS, CHUNKS, 4)),
         ],
         compiler_params=pltpu.CompilerParams(
-            collective_id=0, has_side_effects=True, vmem_limit_bytes=60 * 2**20
+            collective_id=0, has_side_effects=True, vmem_limit_bytes=48 * 2**20
         ),
-    )(right_side, schur, neumann, weights, neighbours, counts, shared_rows)
+    )(*in_hbm(right_side, schur, neumann, weights, neighbours), counts, *in_hbm(shared_rows))
 
 
 def solution(mesh):

time: 56 us -> 53.8 us (0.961)
  Pallas kernels: 53.3 us -> 52.2 us
  local copies, waits for them, and re-layouts: 1.87 us -> 0.8 us
    pallas_call x1, Pallas kernels: 53.3 us -> 52.2 us  [body(): pl.pallas_call(functools.partial(kernel, n), out_shape=jax.ShapeDtypeStru...]
    unnamed x1, local copies, waits for them, and re-layouts: 1.87 us -> 0.8 us
where the time goes in v3:
time: 53.8 us; the launch traced here: 53.6 us
  Pallas kernels  52.2 us (97%)
  local copies, waits for them, and re-layouts  0.8 us (1%)
  between operations  0.66 us (1%)
    pallas_call x1, Pallas kernels, body(): pl.pallas_call(functools.partial(kernel, n), out_shape=jax.ShapeDtypeStru...  52.2 us

profile of v3, /device:TPU:24, one launch (start us, length us, event | category | flops | bytes accessed | tf_op | source)
XLA Modules:
  0.0 53.6 jit_solution(7256205342609129841)
XLA Ops:
  0.7 52.2 %shard_map.73 = f32[1,1024,128]{2,1,0:T(8,128)S(1)} custom-call(bf16[1,1024,128]{2,1,0:T(8,128)(2,1)} %rhs_hbm.1, bf16[1,1024,1024]{2,1,0:T(8,128)(2,1)} %s_hbm.1, bf16[1,1024,1024]{2,1,0:T(8,128)(2,1)} %n_hbm.1, f32[1,1024]{1,0:T(1,128)} %w_hbm.1, s32[1,4]{1,0:T(1,128)} %nb_hbm.1, s32[1]{0:T(128)S(6)} %copy.9.cnt_hbm, s32[1,4,128]{2,1,0:T(4,128)} %rows_hbm.1), custom_call_target="tpu_custom_call" | custom-call | tf_op jit(solution)/shard_map/pallas_call | solution.py:194
  52.9 0.8 %copy.10 = f32[1,1024,128]{2,1,0:T(8,128)} copy(f32[1,1024,128]{2,1,0:T(8,128)S(1)} %shard_map.73) | data formatting | bytes 1048576

commit v4 on v3

--- a/solution.py
+++ b/solution.py
@@ -56,10 +56,10 @@
     for copy in loads:
         copy.start()
 
-    step_rows = leads // CHUNKS
+    cuts = (0, 48, leads)
 
     def copy_of(e, c, slot, there):
-        rows = pl.ds(c * step_rows, step_rows)
+        rows = pl.ds(cuts[c], cuts[c + 1] - cuts[c])
         return pltpu.make_async_remote_copy(
             src_ref=send.at[e, slot, rows],
             dst_ref=recv.at[e, there, rows],
@@ -77,7 +77,7 @@
 
     def put(e, c, rows, slots=range(4)):
         for i, slot in enumerate(slots):
-            send[e, slot, pl.ds(c * step_rows, step_rows)] = rows[:, i * share : (i + 1) * share]
+            send[e, slot, cuts[c] : cuts[c + 1]] = rows[:, i * share : (i + 1) * share]
 
     def got(e, lo, hi):
         return jnp.concatenate([recv[e, slot, lo:hi] for slot in range(4)], axis=1)
@@ -91,7 +91,7 @@
     rhs[...] = jnp.transpose(rhs_in[...])
     p0[...] = mm(rhs[...], pick[...])
     for c in range(CHUNKS):
-        put(0, c, p0[c * step_rows : (c + 1) * step_rows].astype(BF16))
+        put(0, c, p0[cuts[c] : cuts[c + 1]].astype(BF16))
     pl.semaphore_wait(barrier, sum(jnp.where(there, 1, 0) for there in exists))
     for c in range(CHUNKS):
         start(0, c)
@@ -133,7 +133,7 @@
     x[...] = jnp.zeros_like(x)
 
     def spans():
-        return [(c, c * step_rows, (c + 1) * step_rows) for c in range(CHUNKS)]
+        return [(c, cuts[c], cuts[c + 1]) for c in range(CHUNKS)]
 
     halves = [((0, 1), slice(0, 2 * share)), ((2, 3), slice(2 * share, 4 * share))]
 

time: 53.8 us -> 54.2 us (level)
  no operation moved by 1% of the time
where the time goes in v4:
time: 54.2 us; the launch traced here: 54 us
  Pallas kernels  52.6 us (97%)
  local copies, waits for them, and re-layouts  0.8 us (1%)
  between operations  0.66 us (1%)
    pallas_call x1, Pallas kernels, body(): pl.pallas_call(functools.partial(kernel, n), out_shape=jax.ShapeDtypeStru...  52.6 us

profile of v4, /device:TPU:24, one launch (start us, length us, event | category | flops | bytes accessed | tf_op | source)
XLA Modules:
  0.0 54.0 jit_solution(11918196624460244318)
XLA Ops:
  0.7 52.6 %shard_map.73 = f32[1,1024,128]{2,1,0:T(8,128)S(1)} custom-call(bf16[1,1024,128]{2,1,0:T(8,128)(2,1)} %rhs_hbm.1, bf16[1,1024,1024]{2,1,0:T(8,128)(2,1)} %s_hbm.1, bf16[1,1024,1024]{2,1,0:T(8,128)(2,1)} %n_hbm.1, f32[1,1024]{1,0:T(1,128)} %w_hbm.1, s32[1,4]{1,0:T(1,128)} %nb_hbm.1, s32[1]{0:T(128)S(6)} %copy.9.cnt_hbm, s32[1,4,128]{2,1,0:T(4,128)} %rows_hbm.1), custom_call_target="tpu_custom_call" | custom-call | tf_op jit(solution)/shard_map/pallas_call | solution.py:194
  53.2 0.8 %copy.10 = f32[1,1024,128]{2,1,0:T(8,128)} copy(f32[1,1024,128]{2,1,0:T(8,128)S(1)} %shard_map.73) | data formatting | bytes 1048576
